TPU v7x, 256 devices: a whole 4x4x8 slice. The times are simulated.
256 devices in a mesh: space: 32 (over y, z_hi, core), test: 2 (over z_lo), trial: 4 (over x).
Axes of the slice: x: 4, y: 4, z: 8 (z_hi: 4, z_lo: 2; z = z_hi * 2 + z_lo), core: 2. Of those that a mesh axis runs over, the one named last changes fastest.
Arguments:
- test_modes: bfloat16 [3, 128, 128, 8, 128], P(None, 'test', 'space'), may hold values from -6 to 6
- trial_modes: bfloat16 [3, 128, 128, 8, 128], P(None, 'trial', 'space'), may hold values from -6 to 6
- volumes: float32 [128, 8, 128], P('space'), may hold values from 0.25 to 4
Outputs:
- tensor: float32 [128, 128, 128], P('space', 'test', 'trial')
All inputs are finite; a program needn't handle non-finite values.
Results may differ from a plain program's by a relative error of at most 0.0051.
Values may be sent and summed in bfloat16 or wider, within the bound.
No kernel may reach another device: no remote copies, remote signals or barrier semaphores. Data moves between devices by JAX's collectives and lax.ppermute only.
A program may use at most 64 MiB of HBM per device.

v0:
```python
import math
import jax
import jax.numpy as jnp
from jax import lax
from jax.sharding import PartitionSpec as P


def with_halo(cells, sides, width):
    for axis, dim in sides:
        count = lax.axis_size(axis)
        ends = count - 1
        head = lax.slice_in_dim(cells, 0, width, axis=dim)
        tail = lax.slice_in_dim(cells, cells.shape[dim] - width, cells.shape[dim], axis=dim)
        cells = jnp.concatenate(
            [
                lax.ppermute(tail, axis, [(i, (i + 1) % count) for i in range(ends)]),
                cells,
                lax.ppermute(head, axis, [((i + 1) % count, i) for i in range(ends)]),
            ],
            axis=dim,
        )
    return cells


def derivatives(padded):
    field = padded.astype(jnp.float32)
    along_x = (field[:, :, 2:] - field[:, :, :-2]) * 0.5
    center = field[:, :, 1:-1]
    wide_y = jnp.pad(center, ((0, 0), (0, 0), (0, 0), (1, 1), (0, 0)))
    along_y = (wide_y[:, :, :, 2:] - wide_y[:, :, :, :-2]) * 0.5
    wide_z = jnp.pad(center, ((0, 0), (0, 0), (0, 0), (0, 0), (1, 1)))
    along_z = (wide_z[:, :, :, :, 2:] - wide_z[:, :, :, :, :-2]) * 0.5
    return jnp.stack([along_x, along_y, along_z], axis=1).astype(jnp.bfloat16)


def pick_row(array, plane, row, first):
    return lax.dynamic_index_in_dim(
        lax.dynamic_index_in_dim(array, plane, first, False), row, first, False
    )


def block_terms(mode_rows, grad_rows, weighted):
    width_j = mode_rows.shape[1]
    width_k = grad_rows.shape[2]
    planes = mode_rows.shape[2]
    rows_each = mode_rows.shape[3]

    def advance(position, running):
        plane = position // rows_each
        row = position % rows_each
        trial_block = pick_row(mode_rows, plane, row, 2)
        grad_block = pick_row(grad_rows, plane, row, 3)
        test_block = pick_row(weighted, plane, row, 2)
        convected = jnp.einsum(
            "bjc,abkc->ajkc", trial_block, grad_block, preferred_element_type=jnp.float32
        ).astype(jnp.bfloat16)
        return running + jnp.einsum(
            "aic,ajkc->jik", test_block, convected, preferred_element_type=jnp.float32
        )

    running = jnp.zeros((width_j, weighted.shape[1], width_k), jnp.float32)
    return lax.fori_loop(0, planes * rows_each, advance, running)


def finish(partial_value, factor):
    return lax.psum_scatter(partial_value, "space", scatter_dimension=0, tiled=True) * factor


def shards(test_modes, trial_modes, volumes):
    cell_count = trial_modes.shape[2] * trial_modes.shape[3] * trial_modes.shape[4]
    factor = 1.0 / (4.0 * math.sqrt(cell_count * lax.axis_size("space")))
    padded = with_halo(trial_modes, (("space", 2),), 1)
    gradients = derivatives(padded)
    weighted = (test_modes.astype(jnp.float32) * volumes).astype(jnp.bfloat16)
    all_modes = lax.all_gather(trial_modes, "trial", axis=1, tiled=True)
    partial_value = block_terms(all_modes, gradients, weighted)
    return finish(partial_value, factor)


def solution(mesh):
    return jax.shard_map(
        shards,
        mesh=mesh,
        in_specs=(
            P(None, "test", "space", None, None),
            P(None, "trial", "space", None, None),
            P("space", None, None),
        ),
        out_specs=P("space", "test", "trial"),
        check_vma=False,
    )
```

profile of v0, /device:TPU:2, one launch (start us, length us, event | category | flops | bytes accessed | tf_op | source)
XLA Modules:
  0.0 535.8 jit_solution(14520357436832206297)
XLA Ops:
  21.6 31.8 %all-gather.2.cloned.1.call-done = bf16[3,128,4,8,128]{4,1,0,3,2:T(8,128)(2,1)} async-done(((bf16[3,32,4,8,128]{4,1,0,3,2:T(8,128)(2,1)}), bf16[3,128,4,8,128]{4,1,0,3,2:T(8,128)(2,1)}) %all-gather.2.cloned.1.call-update) | async-done | bytes 3145744 | tf_op jit(solution)/shard_map/all_gather | solution.py:75
  53.4 376.8 %while.17 = (s32[]{:T(128)}, f32[128,64,32]{0,1,2:T(8,128)}, bf16[3,3,32,4,8,128]{5,2,1,0,4,3:T(8,128)(2,1)}, bf16[3,128,4,8,128]{4,1,0,3,2:T(8,128)(2,1)}, bf16...) while((s32[]{:T(128)}, f32[128,64,32]{0,1,2:T(8,128)}, ...), condition=%wide.region_1.2_spmd.clone, body=%wide.region_0.1_spmd.clone.sunk | while | flops 211288080 | bytes 15589742 | solution.py:62
  58.0 3.8 copy.26
  81.1 3.8 copy.26
  92.9 3.8 copy.26
  104.7 3.8 copy.26
  116.5 3.8 copy.26
  128.3 3.8 copy.26
  140.1 3.8 copy.26
  151.9 3.8 copy.26
  163.7 3.8 copy.26
  175.5 3.8 copy.26
  187.3 3.8 copy.26
  199.0 3.8 copy.26
  210.8 3.8 copy.26
  222.6 3.8 copy.26
  234.4 3.8 copy.26
  246.2 3.8 copy.26
  269.8 3.8 copy.26
  281.6 3.8 copy.26
  305.1 3.8 copy.26
  316.9 3.8 copy.26
  328.7 3.8 copy.26
  340.5 3.8 copy.26
  352.3 3.8 copy.26
  364.1 3.8 copy.26
  375.9 3.8 copy.26
  387.7 3.8 copy.26
  399.5 3.8 copy.26
  411.3 3.8 copy.26
  430.2 4.0 copy.15
  434.2 93.2 %reduce-scatter.2.cloned.1.call-done = f32[4,64,32]{1,2,0:T(8,128)} async-done(((f32[128,64,32]{1,2,0:T(8,128)}), f32[4,64,32]{1,2,0:T(8,128)}) %reduce-scatter.2.cloned.1.call-update) | async-done | bytes 32784 | tf_op jit(solution)/shard_map/reduce_scatter | solution.py:66
  (219 shorter events, 286.4 us)
Async XLA Ops:
  6.5 6.7 %copy-start.1 = (bf16[3,64,4,8,128]{4,3,2,1,0:T(8,128)(2,1)S(1)}, bf16[3,64,4,8,128]{4,3,2,1,0:T(8,128)(2,1)}, u32[]{:S(2)}) copy-start(bf16[3,64,4,8,128]{4,3,2,1,0:T(8,128)(2,1)} %param.5) | copy-start | bytes 4718596
  6.5 6.7 %copy-start.2 = (f32[4,8,128]{2,1,0:T(8,128)S(1)}, f32[4,8,128]{2,1,0:T(8,128)}, u32[]{:S(2)}) copy-start(f32[4,8,128]{2,1,0:T(8,128)} %param.7) | copy-start | bytes 49156
  6.5 46.8 %all-gather.2.cloned.1.call-start = ((), (), s32[]{:S(2)}) async-start(), calls=%async_computation.1 | async-start | bytes 3932160 | tf_op jit(solution)/shard_map/all_gather | solution.py:75
  9.0 518.5 %reduce-scatter.2.cloned.1.call-start = ((), (), s32[]{:S(2)}) async-start(), calls=%async_computation.2 | async-start | bytes 2162688 | tf_op jit(solution)/shard_map/reduce_scatter | solution.py:66
  10.1 5.0 collective-permute-start
  11.9 6.4 %collective-permute-start.1 = (bf16[3,32,1,8,128]{4,1,0,3,2:T(8,128)(2,1)S(1)}, bf16[3,32,1,8,128]{4,1,0,3,2:T(8,128)(2,1)S(1)}, u32[]{:S(2)}, u32[]{:S(2)}) collective-permute-start(bf16[3,32,1,8,128]{4,1,0,3,2:T(8,128)(2,1)S(1)} %get-tuple-element.203), channel_id=1, source_target_pairs={{8,0},{16,8},{24,16},{32,24},{40,32},{48,40},{56,48},{64,56},{72,6... | collective-permute-start | bytes 589832 | tf_op jit(solution)/shard_map/ppermute | solution.py:18
  13.2 5.1 copy-start
Sparse Core Ops, SparseCore 0:
  9.1 44.1 all-gather.1
  434.4 93.0 reduce-scatter.1
where the time goes:
time: 541 us; the launch traced here: 536 us
  local copies, waits for them, and re-layouts  198 us (37%)
  matrix products  186 us (34%)
  waiting for transfers between devices  128 us (24%)
  between operations  13.5 us (2%)
  other arithmetic  6.63 us (1%)
    dot_general x32, local copies, waits for them, and re-layouts, advance(): jnp.einsum('bjc,abkc->ajkc', trial_block, grad_block, preferred_element_t...  121 us
    dot_general x32, matrix products, advance(): jnp.einsum('aic,ajkc->jik', test_block, convected, preferred_element_type...  106 us
    reduce_scatter x1, waiting for transfers between devices, finish(): lax.psum_scatter(partial_value, 'space', scatter_dimension=0, tiled=True)  93.2 us
    dot_general x32, matrix products, advance(): jnp.einsum('bjc,abkc->ajkc', trial_block, grad_block, preferred_element_t...  79.3 us
    squeeze x128, local copies, waits for them, and re-layouts, pick_row(): lax.dynamic_index_in_dim(lax.dynamic_index_in_dim(array, plane, first, Fa...  69.2 us
    all_gather x1, waiting for transfers between devices, shards(): all_modes = lax.all_gather(trial_modes, 'trial', axis=1, tiled=True)  31.8 us
  transfers between devices with their start and end apart: 4, of which 3 were waited for; matrix products, arithmetic and copies ran while one was open for 1% of the time, Pallas kernels for 0%

commit v1 on v0

--- a/solution.py
+++ b/solution.py
@@ -72,7 +72,9 @@
     padded = with_halo(trial_modes, (("space", 2),), 1)
     gradients = derivatives(padded)
     weighted = (test_modes.astype(jnp.float32) * volumes).astype(jnp.bfloat16)
-    all_modes = lax.all_gather(trial_modes, "trial", axis=1, tiled=True)
+    all_modes = jnp.concatenate(
+        lax.all_to_all(jnp.stack([trial_modes] * lax.axis_size("trial")), "trial", 0, 0), axis=1
+    )
     partial_value = block_terms(all_modes, gradients, weighted)
     return finish(partial_value, factor)
 

time: 541 us -> 371 us (0.69)
  local copies, waits for them, and re-layouts: 198 us -> 100 us
  matrix products: 186 us -> 116 us
  waiting for transfers between devices: 128 us -> 120 us
  starting transfers between devices: 3.09 us -> 10.2 us
    dot_general x32 -> x0, local copies, waits for them, and re-layouts: 121 us -> none  [advance(): jnp.einsum('bjc,abkc->ajkc', trial_block, grad_block, preferred_element_t...]
    while x0 -> x128, local copies, waits for them, and re-layouts: none -> 46.3 us
    dot_general x32, matrix products: 79.3 us -> 42.3 us  [advance(): jnp.einsum('bjc,abkc->ajkc', trial_block, grad_block, preferred_element_t...]
    dot_general x32, matrix products: 106 us -> 73.7 us  [advance(): jnp.einsum('aic,ajkc->jik', test_block, convected, preferred_element_type...]
    all_gather x1 -> x0, waiting for transfers between devices: 31.8 us -> none  [shards(): all_modes = lax.all_gather(trial_modes, 'trial', axis=1, tiled=True)]
    squeeze x128, local copies, waits for them, and re-layouts: 69.2 us -> 40.6 us  [pick_row(): lax.dynamic_index_in_dim(lax.dynamic_index_in_dim(array, plane, first, Fa...]
    all_to_all x0 -> x1, waiting for transfers between devices: none -> 24.2 us  [shards(): lax.all_to_all(jnp.stack([trial_modes] * lax.axis_size('trial')), 'trial'...]
    all_to_all x0 -> x1, starting transfers between devices: none -> 6.97 us  [shards(): lax.all_to_all(jnp.stack([trial_modes] * lax.axis_size('trial')), 'trial'...]
where the time goes in v1:
time: 371 us; the launch traced here: 369 us
  waiting for transfers between devices  120 us (32%)
  matrix products  116 us (31%)
  local copies, waits for them, and re-layouts  100 us (27%)
  between operations  13.5 us (4%)
  starting transfers between devices  10.2 us (3%)
  other arithmetic  6.09 us (2%)
    reduce_scatter x1, waiting for transfers between devices, finish(): lax.psum_scatter(partial_value, 'space', scatter_dimension=0, tiled=True)  94.5 us
    dot_general x32, matrix products, advance(): jnp.einsum('aic,ajkc->jik', test_block, convected, preferred_element_type...  73.7 us
    while x128, local copies, waits for them, and re-layouts  46.3 us
    dot_general x32, matrix products, advance(): jnp.einsum('bjc,abkc->ajkc', trial_block, grad_block, preferred_element_t...  42.3 us
    squeeze x128, local copies, waits for them, and re-layouts, pick_row(): lax.dynamic_index_in_dim(lax.dynamic_index_in_dim(array, plane, first, Fa...  40.6 us
    all_to_all x1, waiting for transfers between devices, shards(): lax.all_to_all(jnp.stack([trial_modes] * lax.axis_size('trial')), 'trial'...  24.2 us
  transfers between devices with their start and end apart: 4, of which 3 were waited for; matrix products, arithmetic and copies ran while one was open for 1% of the time, Pallas kernels for 0%

profile of v1, /device:TPU:2, one launch (start us, length us, event | category | flops | bytes accessed | tf_op | source)
XLA Modules:
  0.0 369.3 jit_solution(12668376838836254584)
XLA Ops:
  8.0 2.3 stack.27
  10.3 7.0 %all-to-all-start = ((bf16[4,3,32,4,8,128]{5,2,1,4,3,0:T(8,128)(2,1)}), bf16[4,3,32,4,8,128]{5,2,1,4,3,0:T(8,128)(2,1)}, u32[]{:S(2)}, u32[]{:S(2)}) async-start(bf16[4,3,32,4,8,128]{5,2,1,4,3,0:T(8,128)(2,1)} %stack.27), calls=%async_computation | async-start | bytes 6291456 | tf_op jit(solution)/shard_map/all_to_all | solution.py:76
  27.7 24.2 %all-to-all-done = bf16[4,3,32,4,8,128]{5,2,1,4,3,0:T(8,128)(2,1)} async-done(((bf16[4,3,32,4,8,128]{5,2,1,4,3,0:T(8,128)(2,1)}), bf16[4,3,32,4,8,128]{5,2,1,4,3,0:T(8,128)(2,1)}, u32[]{:S(2)}, u32[]{:S(2)}) %all-to-all-start) | async-done | bytes 3145760 | tf_op jit(solution)/shard_map/all_to_all | solution.py:76
  51.9 3.1 copy.36
  55.0 2.8 copy.38
  57.8 205.9 %while.17 = (s32[]{:T(128)}, f32[128,64,32]{0,1,2:T(8,128)S(1)}, bf16[3,3,32,4,8,128]{5,2,1,0,4,3:T(8,128)(2,1)S(1)}, bf16[3,128,4,8,128]{4,1,0,3,2:T(8,128)(2,1...) while((s32[]{:T(128)}, f32[128,64,32]{0,1,2:T(8,128)S(1)}, ...), condition=%wide.region_1.2_spmd.clone, body=%wide.region_0.1_spmd.clone.sunk | while | flops 212860944 | bytes 28172716 | solution.py:62
  61.9 2.3 fusion.34
  68.4 2.3 fusion.34
  74.8 2.3 fusion.34
  81.2 2.3 fusion.34
  87.7 2.3 fusion.34
  94.1 2.3 fusion.34
  107.0 2.3 fusion.34
  113.4 2.3 fusion.34
  119.8 2.3 fusion.34
  132.7 2.3 fusion.34
  152.0 2.3 fusion.34
  158.4 2.3 fusion.34
  164.9 2.3 fusion.34
  171.3 2.3 fusion.34
  177.7 2.3 fusion.34
  190.6 2.3 fusion.34
  203.5 2.3 fusion.34
  209.9 2.3 fusion.34
  216.3 2.3 fusion.34
  222.8 2.3 fusion.34
  229.2 2.3 fusion.34
  235.6 2.3 fusion.34
  248.5 2.3 fusion.34
  261.4 2.3 fusion.34
  263.7 2.8 copy.39
  266.5 94.5 %reduce-scatter.2.cloned.1.call-done = f32[4,64,32]{1,2,0:T(8,128)} async-done(((f32[128,64,32]{1,2,0:T(8,128)}), f32[4,64,32]{1,2,0:T(8,128)}) %reduce-scatter.2.cloned.1.call-update) | async-done | bytes 32784 | tf_op jit(solution)/shard_map/reduce_scatter | solution.py:66
  (315 shorter events, 160.9 us)
Async XLA Ops:
  10.3 11.1 %copy-start.2 = (bf16[3,64,4,8,128]{4,3,2,1,0:T(8,128)(2,1)S(1)}, bf16[3,64,4,8,128]{4,3,2,1,0:T(8,128)(2,1)}, u32[]{:S(2)}) copy-start(bf16[3,64,4,8,128]{4,3,2,1,0:T(8,128)(2,1)} %param.5) | copy-start | bytes 4718596
  10.3 11.1 %copy-start.3 = (f32[4,8,128]{2,1,0:T(8,128)S(1)}, f32[4,8,128]{2,1,0:T(8,128)}, u32[]{:S(2)}) copy-start(f32[4,8,128]{2,1,0:T(8,128)} %param.7) | copy-start | bytes 49156
  10.3 41.6 %all-to-all-start = ((bf16[4,3,32,4,8,128]{5,2,1,4,3,0:T(8,128)(2,1)}), bf16[4,3,32,4,8,128]{5,2,1,4,3,0:T(8,128)(2,1)}, u32[]{:S(2)}, u32[]{:S(2)}) async-start(bf16[4,3,32,4,8,128]{5,2,1,4,3,0:T(8,128)(2,1)} %stack.27), calls=%async_computation | async-start | bytes 6291456 | tf_op jit(solution)/shard_map/all_to_all | solution.py:76
  17.3 343.7 %reduce-scatter.2.cloned.1.call-start = ((), (), s32[]{:S(2)}) async-start(), calls=%async_computation.2 | async-start | bytes 2162688 | tf_op jit(solution)/shard_map/reduce_scatter | solution.py:66
  18.1 5.1 %collective-permute-start = (bf16[3,32,1,8,128]{4,1,0,3,2:T(8,128)(2,1)}, bf16[3,32,1,8,128]{4,1,0,3,2:T(8,128)(2,1)}, u32[]{:S(2)}, u32[]{:S(2)}) collective-permute-start(bf16[3,32,1,8,128]{4,1,0,3,2:T(8,128)(2,1)} %get-tuple-element.207), channel_id=1, source_target_pairs={{0,8},{8,16},{16,24},{24,32},{32,40},{40,48},{48,56},{56,64},{64,7... | collective-permute-start | bytes 589832 | tf_op jit(solution)/shard_map/ppermute | solution.py:16
  20.0 4.8 %collective-permute-start.1 = (bf16[3,32,1,8,128]{4,1,0,3,2:T(8,128)(2,1)}, bf16[3,32,1,8,128]{4,1,0,3,2:T(8,128)(2,1)}, u32[]{:S(2)}, u32[]{:S(2)}) collective-permute-start(bf16[3,32,1,8,128]{4,1,0,3,2:T(8,128)(2,1)} %get-tuple-element.208), channel_id=1, source_target_pairs={{8,0},{16,8},{24,16},{32,24},{40,32},{48,40},{56,48},{64,56},{72,6... | collective-permute-start | bytes 589832 | tf_op jit(solution)/shard_map/ppermute | solution.py:18
  61.9 2.3 copy-start.1
  68.3 2.3 copy-start.1
  74.8 2.3 copy-start.1
  81.2 2.3 copy-start.1
  87.6 2.3 copy-start.1
  94.1 2.3 copy-start.1
  100.5 2.3 copy-start.1
  106.9 2.3 copy-start.1
  113.4 2.3 copy-start.1
  119.8 2.3 copy-start.1
  126.2 2.3 copy-start.1
  132.7 2.3 copy-start.1
  152.0 2.3 copy-start.1
  158.4 2.3 copy-start.1
  164.9 2.3 copy-start.1
  171.3 2.3 copy-start.1
  177.7 2.3 copy-start.1
  190.6 2.3 copy-start.1
  203.5 2.3 copy-start.1
  209.9 2.3 copy-start.1
  216.3 2.3 copy-start.1
  222.8 2.3 copy-start.1
  229.2 2.3 copy-start.1
  235.6 2.3 copy-start.1
  248.5 2.3 copy-start.1
  261.4 2.3 copy-start.1
  (38 other events, 61.0 us)
Sparse Core Ops, SparseCore 0:
  266.7 94.2 reduce-scatter.1
